TPU v7x, 32 devices: a whole 2x2x4 slice. The times are simulated.
32 devices in a mesh: span: 16 (over z, x, core), seq: 2 (over y).
Axes of the slice: x: 2, y: 2, z: 4, core: 2. Of those that a mesh axis runs over, the one named last changes fastest.
Arguments:
- tokens: bfloat16 [8192, 1024], P(('span', 'seq')), may hold values from -48 to 48
- w_qkv: bfloat16 [1024, 3072], P('span'), may hold values from -0.1875 to 0.1875
- w_out: bfloat16 [1024, 1024], replicated, may hold values from -0.1875 to 0.1875
- w_cross: bfloat16 [1024, 2048], replicated, may hold values from -0.1875 to 0.1875
- ln_gain: float32 [1024], replicated, may hold values from 0.5 to 1.5
- ln_bias: float32 [1024], replicated, may hold values from -3 to 3
- queries: bfloat16 [1024, 1024], replicated, may hold values from -144 to 144
Outputs:
- encoded: bfloat16 [8192, 1024], P(('span', 'seq'))
- cross_out: bfloat16 [1024, 1024], P('span')
All inputs are finite; a program needn't handle non-finite values.
Results may differ from a plain program's by a relative error of at most 0.013.
The roundings to bfloat16 on the way count: a program that leaves them out, or rounds other values in their place, can miss the bound.
Values may be sent and summed in bfloat16 or wider, within the bound.
A program may use at most 128 MiB of HBM per device.

v0:
```python
import jax
import jax.numpy as jnp
from jax import lax
from jax.sharding import PartitionSpec as P

H = 16
DH = 64


score_scale = 0.125


def layer_norm(residual, ln_gain, ln_bias):
    center = residual - jnp.mean(residual, -1, keepdims=True)
    spread = jnp.mean(center * center, -1, keepdims=True)
    return center * lax.rsqrt(spread + 1e-05) * ln_gain + ln_bias


def per_device(tokens, w_qkv, w_out, w_cross, ln_gain, ln_bias, queries):
    tok_rows = tokens.shape[0]
    model_width = tokens.shape[1]
    seq_count = lax.axis_size("seq")
    span_count = lax.axis_size("span")
    projected = jnp.dot(
        tokens,
        lax.all_gather(w_qkv, "span", axis=0, tiled=True),
        preferred_element_type=jnp.float32,
    )
    projected = projected.astype(jnp.bfloat16).reshape(tok_rows, 3, model_width)
    grouped = lax.all_to_all(projected, "seq", split_axis=2, concat_axis=0, tiled=True)
    span_length = tok_rows * seq_count
    heads_here = grouped.shape[2] // DH
    query_all = grouped[:, 0].reshape(span_length, heads_here, DH)
    key_all = grouped[:, 1].reshape(span_length, heads_here, DH)
    value_all = grouped[:, 2].reshape(span_length, heads_here, DH)
    block_rows = min(512, span_length)
    query_blocks = query_all.reshape(span_length // block_rows, block_rows, heads_here, DH)

    def attend(query_block):
        scores = (
            jnp.einsum("qhd,khd->hqk", query_block, key_all, preferred_element_type=jnp.float32)
            * score_scale
        )
        peaks = jnp.max(scores, -1, keepdims=True)
        powers = jnp.exp(scores - peaks)
        totals = jnp.sum(powers, -1, keepdims=True)
        mixed = jnp.einsum(
            "hqk,khd->qhd",
            powers.astype(jnp.bfloat16),
            value_all,
            preferred_element_type=jnp.float32,
        )
        mixed = mixed / jnp.transpose(totals, (1, 0, 2))
        return mixed.astype(jnp.bfloat16).reshape(block_rows, heads_here * DH)

    attn = lax.map(attend, query_blocks).reshape(span_length, heads_here * DH)
    attn_tokens = lax.all_to_all(attn, "seq", split_axis=0, concat_axis=1, tiled=True)
    residual = tokens.astype(jnp.float32) + jnp.dot(
        attn_tokens, w_out, preferred_element_type=jnp.float32
    )
    encoded = layer_norm(residual, ln_gain, ln_bias).astype(jnp.bfloat16)
    cross_kv = jnp.dot(encoded, w_cross, preferred_element_type=jnp.float32).astype(jnp.bfloat16)
    cross_keys = cross_kv[:, :model_width].reshape(tok_rows, H, DH)
    cross_values = cross_kv[:, model_width:].reshape(tok_rows, H, DH)
    query_count = queries.shape[0]
    query_heads = queries.reshape(query_count, H, DH)
    cross_scores = (
        jnp.einsum("qhd,khd->qhk", query_heads, cross_keys, preferred_element_type=jnp.float32)
        * score_scale
    )
    local_peak = jnp.max(cross_scores, -1)
    cross_peak = lax.pmax(local_peak, ("span", "seq"))
    cross_powers = jnp.exp(cross_scores - cross_peak[:, :, None])
    cross_total = jnp.sum(cross_powers, -1)
    numerator = jnp.einsum(
        "qhk,khd->qhd",
        cross_powers.astype(jnp.bfloat16),
        cross_values,
        preferred_element_type=jnp.float32,
    )
    numerator = numerator.reshape(query_count, model_width)
    own_rows = query_count // span_count
    summed, sum_total = lax.psum((numerator, cross_total), ("span", "seq"))
    row_start = lax.axis_index("span") * own_rows
    summed = lax.dynamic_slice_in_dim(summed, row_start, own_rows, 0)
    sum_total = lax.dynamic_slice_in_dim(sum_total, row_start, own_rows, 0)
    cross_out = summed.reshape(own_rows, H, DH) / sum_total[:, :, None]
    return (encoded, cross_out.reshape(own_rows, model_width).astype(jnp.bfloat16))


def solution(mesh):
    in_specs = (P(("span", "seq"), None), P("span", None), P(), P(), P(), P(), P())
    out_specs = (P(("span", "seq"), None), P("span", None))
    return jax.shard_map(
        per_device, mesh=mesh, in_specs=in_specs, out_specs=out_specs, check_vma=False
    )
```

profile of v0, /device:TPU:27, one launch (start us, length us, event | category | flops | bytes accessed | tf_op | source)
XLA Modules:
  0.0 450.9 jit_solution(16979895533489003373)
XLA Ops:
  7.2 0.0 copy-start
  7.2 0.0 all-gather.2.cloned.1.call-start
  7.2 0.7 all-gather.2.cloned.1.call-update
  7.9 62.9 %all-gather.2.cloned.1.call-done = bf16[1024,3072]{1,0:T(8,128)(2,1)} async-done(((bf16[64,3072]{1,0:T(8,128)(2,1)}), bf16[1024,3072]{1,0:T(8,128)(2,1)}) %all-gather.2.cloned.1.call-update) | async-done | bytes 6291472 | tf_op jit(solution)/shard_map/all_gather | solution.py:26
  70.9 5.9 %convolution_convert_fusion = bf16[256,3072]{1,0:T(8,128)(2,1)} fusion(bf16[256,1024]{1,0:T(8,128)(2,1)} %param.7, bf16[1024,3072]{1,0:T(8,128)(2,1)} %all-gather.2.cloned.1.call-done), kind=kOutput, calls=%fused_computation.15 | convolution fusion | flops 1611399168 | bytes 8388608 | tf_op jit(solution)/shard_map/dot_general | solution.py:24
  76.8 2.6 copy.36
  79.4 2.8 copy.37
  82.1 27.2 %all_to_all.37 = bf16[256,3,1024]{0,1,2:T(4,128)(2,1)S(1)} all-to-all(bf16[256,3,1024]{0,1,2:T(4,128)(2,1)S(1)} %copy.37), channel_id=1, replica_groups=mesh['span'=16,'seq'=2] {'seq'}, dimensions={2} | all-to-all | bytes 3145728 | tf_op jit(solution)/shard_map/all_to_all | solution.py:30
  109.3 1.4 copy.38
  110.7 2.6 copy.39
  113.4 2.3 fusion.20
  115.6 1.0 copy.40
  116.6 0.2 copy.41
  116.8 1.3 copy.42
  118.1 1.3 multiply_reduce_fusion
  119.4 1.4 fusion.7
  120.8 0.0 copy-done.3
  120.8 0.0 copy-start.1
  120.8 2.4 divide_convert_fusion
  123.2 1.2 all_to_all.31
  124.4 0.9 copy.44
  125.2 3.5 all-to-all-start.1
  128.7 0.2 all-reduce.4.cloned.1.call-start
  129.0 4.0 copy.47
  132.9 2.7 all-to-all-done.1
  135.7 0.0 copy-done
  135.7 0.8 fusion.22
  136.5 0.3 multiply_reduce_fusion.1
  136.8 0.2 add_convert_fusion
  137.1 0.0 copy-start.2
  137.1 3.7 convolution_convert_fusion.1
  140.7 0.9 fusion.21
  141.6 1.2 copy.46
  142.8 10.3 %bitcast_reduce_fusion = (f32[1024,16]{0,1:T(8,128)}, f32[16,256,1024]{2,1,0:T(8,128)}) fusion(bf16[256,16,64]{0,2,1:T(8,128)(2,1)S(1)} %bitcast.58, bf16[1024,16,64]{0,2,1:T(8,128)(2,1)} %bitcast.51), kind=kOutput, calls=%fused_computation.1 | convolution fusion | flops 545243136 | bytes 19464192 | tf_op jit(solution)/shard_map/qhd,khd->qhk/dot_general | solution.py:68
  153.2 0.0 all-reduce.4.cloned.1.call-update
  153.2 0.0 all-reduce.6.cloned.1.call-start
  153.2 0.2 copy.45
  153.4 121.5 %all-reduce.4.cloned.1.call-done = f32[1024,16]{0,1:T(8,128)} async-done(((f32[1024,16]{0,1:T(8,128)}), f32[1024,16]{0,1:T(8,128)}) %all-reduce.4.cloned.1.call-update) | async-done | bytes 65552 | tf_op jit(solution)/shard_map/pmax | solution.py:72
  274.9 10.7 %fusion.3 = f32[16,64,1024]{2,1,0:T(8,128)} fusion(bf16[256,16,64]{0,2,1:T(8,128)(2,1)S(1)} %bitcast.59, f32[16,256,1024]{2,1,0:T(8,128)} %get-tuple-element.29, f32[1024,16]{0,1:T(8,128)} %all-reduce.4.cloned.1.call-done), kind=kOutput, calls=%fused_computation.5 | convolution fusion | flops 549453824 | bytes 21561344 | tf_op jit(solution)/shard_map/qhk,khd->qhd/dot_general | solution.py:75
  285.6 5.4 %copy.49 = f32[1024,1024]{1,0:T(8,128)} copy(f32[1024,1024]{0,1:T(8,128)} %bitcast.50) | data formatting | bytes 8388608 | tf_op jit(solution)/shard_map/reshape | solution.py:81
  291.0 9.3 %fusion.1 = f32[1024,16]{0,1:T(8,128)} fusion(f32[16,256,1024]{2,1,0:T(8,128)} %get-tuple-element.29, f32[1024,16]{0,1:T(8,128)S(1)} %copy-done.4), kind=kLoop, calls=%fused_computation.3 | loop fusion | flops 12566528 | bytes 16908288 | tf_op jit(solution)/shard_map/reduce_sum | solution.py:74
  300.2 0.0 all-reduce.6.cloned.1.call-update
  300.3 141.2 %all-reduce.6.cloned.1.call-done = (f32[1024,16]{0,1:T(8,128)}, f32[1024,1024]{1,0:T(8,128)}) async-done(((f32[1024,16]{0,1:T(8,128)}, f32[1024,1024]{1,0:T(8,128)}), (f32[1024,16]{0,1:T(8,128)}, f32[1024,1024]{1,0:T(8,128)})) %all-reduce.6.cloned.1.call-update) | async-done | bytes 4259856 | tf_op jit(solution)/shard_map/psum | solution.py:83
  441.5 0.8 constant_dynamic-slice_fusion
  442.2 0.1 copy.50
  442.3 0.2 div.36
  442.5 0.2 div.37
  442.7 1.7 divide_convert_fusion.1
  (11 shorter events, 0.0 us)
Async XLA Ops:
  7.2 128.5 %copy-start = (bf16[1024,1024]{1,0:T(8,128)(2,1)S(1)}, bf16[1024,1024]{1,0:T(8,128)(2,1)}, u32[]{:S(2)}) copy-start(bf16[1024,1024]{1,0:T(8,128)(2,1)} %param.9) | copy-start | bytes 6291460
  7.2 63.7 %all-gather.2.cloned.1.call-start = ((), (), s32[]{:S(2)}) async-start(), calls=%async_computation.2 | async-start | bytes 6684672 | tf_op jit(solution)/shard_map/all_gather | solution.py:26
  118.1 2.7 copy-start.3
  120.8 14.9 %copy-start.1 = (bf16[256,1024]{1,0:T(8,128)(2,1)S(1)}, bf16[256,1024]{1,0:T(8,128)(2,1)}, u32[]{:S(2)}) copy-start(bf16[256,1024]{1,0:T(8,128)(2,1)} %param.7) | copy-start | bytes 1572868
  123.2 13.6 %copy-start.5 = (f32[1024]{0:T(1024)S(1)}, f32[1024]{0:T(1024)}, u32[]{:S(2)}) copy-start(f32[1024]{0:T(1024)} %param.12) | copy-start | bytes 12292
  123.2 13.6 %copy-start.6 = (f32[1024]{0:T(1024)S(1)}, f32[1024]{0:T(1024)}, u32[]{:S(2)}) copy-start(f32[1024]{0:T(1024)} %param.11) | copy-start | bytes 12292
  125.2 10.4 %all-to-all-start.1 = ((bf16[2,256,512]{1,2,0:T(8,128)(2,1)}), bf16[2,256,512]{1,2,0:T(8,128)(2,1)S(1)}, u32[]{:S(2)}, u32[]{:S(2)}) async-start(bf16[2,256,512]{1,2,0:T(8,128)(2,1)} %copy.44), calls=%async_computation.1 | async-start | bytes 1048576 | tf_op jit(solution)/shard_map/all_to_all | solution.py:57
  128.7 146.2 %all-reduce.4.cloned.1.call-start = ((), (), s32[]{:S(2)}) async-start(), calls=%async_computation.3 | async-start | bytes 131072 | tf_op jit(solution)/shard_map/pmax | solution.py:72
  137.1 4.5 %copy-start.2 = (bf16[256,1024]{1,0:T(8,128)(2,1)}, bf16[256,1024]{1,0:T(8,128)(2,1)S(1)}, u32[]{:S(2)}) copy-start(bf16[256,1024]{1,0:T(8,128)(2,1)S(1)} %add_convert_fusion) | copy-start | bytes 1572868
  153.2 288.3 %all-reduce.6.cloned.1.call-start = ((), (), s32[]{:S(2)}) async-start(), calls=%async_computation.4 | async-start | bytes 8519680 | tf_op jit(solution)/shard_map/psum | solution.py:83
  285.6 5.4 %copy-start.4 = (f32[1024,16]{0,1:T(8,128)S(1)}, f32[1024,16]{0,1:T(8,128)}, u32[]{:S(2)}) copy-start(f32[1024,16]{0,1:T(8,128)} %all-reduce.4.cloned.1.call-done) | copy-start | bytes 196612
Sparse Core Ops, SparseCore 0:
  10.3 60.5 all-gather.1
  153.3 121.5 all-reduce.3
  300.4 141.0 all-reduce.5
where the time goes:
time: 456 us; the launch traced here: 451 us
  waiting for transfers between devices  329 us (72%)
  matrix products  35.1 us (8%)
  local copies, waits for them, and re-layouts  29 us (6%)
  blocking collectives  27.2 us (6%)
  between operations  13.9 us (3%)
  other arithmetic  12.8 us (3%)
    psum x1, waiting for transfers between devices, per_device(): summed, sum_total = lax.psum((numerator, cross_total), ('span', 'seq'))  141 us
    pmax x1, waiting for transfers between devices, per_device(): cross_peak = lax.pmax(local_peak, ('span', 'seq'))  121 us
    all_gather x1, waiting for transfers between devices, per_device(): lax.all_gather(w_qkv, 'span', axis=0, tiled=True)  62.9 us
    all_to_all x1, blocking collectives, per_device(): lax.all_to_all(projected, 'seq', split_axis=2, concat_axis=0, tiled=True)  27.2 us
    dot_general x1, matrix products, per_device(): jnp.einsum('qhk,khd->qhd', cross_powers.astype(jnp.bfloat16), cross_value...  10.7 us
    dot_general x1, matrix products, per_device(): jnp.einsum('qhd,khd->qhk', query_heads, cross_keys, preferred_element_typ...  10.3 us
    reduce_sum x1, other arithmetic, per_device(): cross_total = jnp.sum(cross_powers, -1)  9.28 us
  transfers between devices with their start and end apart: 4, of which 4 were waited for; matrix products, arithmetic and copies ran while one was open for 1% of the time, Pallas kernels for 0%

commit v1 on v0

v1 whole, which is shorter than its diff:
```python
import functools

import jax
import jax.numpy as jnp
from jax import lax
from jax.experimental import pallas as pl
from jax.experimental.pallas import tpu as pltpu
from jax.sharding import PartitionSpec as P

DH = 64
PAIR = 2 * DH
score_scale = 0.125
F32 = jnp.float32
BF16 = jnp.bfloat16
MESH = pl.DeviceIdType.MESH


def mm(a, b):
    return jnp.dot(a, b, preferred_element_type=F32)


def mm_t(a, b):
    return lax.dot_general(a, b, (((1,), (1,)), ((), ())), preferred_element_type=F32)


def pair_attend(query, key, value):
    lane = lax.broadcasted_iota(jnp.int32, (1, PAIR), 1)
    low = lane < DH
    low_f = jnp.where(low, 1.0, 0.0)
    low_b = low_f.astype(BF16)
    high_b = (1.0 - low_f).astype(BF16)
    scaled = query * jnp.asarray(score_scale, BF16)

    def one(own, other):
        scores = mm_t(scaled * own, key)
        peak = jnp.max(scores, -1, keepdims=True)
        probs = jnp.exp(scores - peak).astype(BF16)
        return mm(probs, value * own + other), peak

    first, first_peak = one(low_b, high_b)
    second, second_peak = one(high_b, low_b)
    numerator = jnp.where(low, first, second)
    total = pltpu.roll(jnp.where(low, second, first), DH, 1)
    return numerator, total, jnp.where(low, first_peak, second_peak)


def kernel(
    S, Q, NQ,
    tokens_ref, wqkv_ref, wout_ref, wcross_ref, gain_ref, bias_ref, queries_ref,
    enc_ref, out_ref,
    wbuf, tokall, acc, qkv, wout, wc, qc, attn_tx, attn, res, kv_tx, kv, o_tx, l_tx, o_rx, l_rx,
    local_sem, z_send, z_recv, x_send, x_recv, c_send, c_recv,
    tok_send, tok_recv, at_send, at_recv, kv_send, kv_recv, o_send, o_recv, l_send, l_recv,
):
    T, D = tokens_ref.shape
    R = wqkv_ref.shape[0]
    hcols = D // Q
    Z = S // 4
    G = D // PAIR
    own_rows = NQ // S
    span = lax.axis_index("span")
    seq = lax.axis_index("seq")
    z = span // 4
    x = (span // 2) % 2
    c = span % 2
    member = span % G
    base = span - member
    flat = span * Q + seq

    loads = []

    def load(src, dst):
        copy = pltpu.make_async_copy(src, dst, local_sem.at[len(loads)])
        copy.start()
        loads.append(copy)
        return copy

    own_w = pl.ds(pl.multiple_of(span * R, R), R)
    w_loads = [
        load(
            wqkv_ref.at[:, pl.ds(pl.multiple_of(j * D + seq * hcols, 128), hcols)],
            wbuf.at[own_w, pl.ds(j * hcols, hcols)],
        )
        for j in range(3)
    ]
    own_t = pl.ds(pl.multiple_of(seq * T, T), T)
    t_load = load(tokens_ref, tokall.at[own_t])

    barrier = pltpu.get_barrier_semaphore()
    n = S * Q

    def greet(i, carry):
        other = (flat + i) % n
        pl.semaphore_signal(
            barrier, inc=1, device_id={"span": other // Q, "seq": other % Q}, device_id_type=MESH
        )
        return carry

    lax.fori_loop(1, n, greet, 0)
    wo_load = load(wout_ref, wout)
    wc_loads = []
    for g in range(G):
        for half in range(2):
            wc_loads.append(
                load(
                    wcross_ref.at[:, pl.ds(half * D + g * PAIR, PAIR)],
                    wc.at[g, :, pl.ds(half * PAIR, PAIR)],
                )
            )
    q_load = load(queries_ref.at[:, pl.ds(pl.multiple_of(member * PAIR, PAIR), PAIR)], qc)
    for copy in w_loads:
        copy.wait()
    pl.semaphore_wait(barrier, n - 1)

    def remote(src, dst, ssem, rsem, to_span, to_seq):
        return pltpu.make_async_remote_copy(
            src_ref=src, dst_ref=dst, send_sem=ssem, recv_sem=rsem,
            device_id={"span": to_span, "seq": to_seq}, device_id_type=MESH,
        )

    def block(zz, xx, cc):
        return wbuf.at[pl.ds(pl.multiple_of((zz * 4 + xx * 2 + cc) * R, R), R)]

    x_peer = z * 4 + (1 - x) * 2 + c
    c_peer = z * 4 + x * 2 + (1 - c)
    sent = []

    def send(copy):
        copy.start()
        sent.append(copy)

    def to_x(zz):
        b = block(zz, x, c)
        return remote(b, b, x_send.at[zz], x_recv.at[zz], x_peer, seq)

    def from_x(zz):
        b = block(zz, 1 - x, c)
        return remote(b, b, x_send.at[zz], x_recv.at[zz], x_peer, seq)

    def to_c(zz, xx):
        b = block(zz, xx, c)
        return remote(b, b, c_send.at[zz * 2 + xx], c_recv.at[zz * 2 + xx], c_peer, seq)

    def from_c(zz, xx):
        b = block(zz, xx, 1 - c)
        return remote(b, b, c_send.at[zz * 2 + xx], c_recv.at[zz * 2 + xx], c_peer, seq)

    def at_z(k):
        return (z + k) % Z

    order = [0]
    for d in range(1, Z // 2 + 1):
        for k in (d, Z - d):
            if k not in order:
                order.append(k)
    send(to_x(z))
    send(to_c(z, x))
    for k in order[1:]:
        b = block(z, x, c)
        send(remote(b, b, z_send.at[k], z_recv.at[z], at_z(k) * 4 + x * 2 + c, seq))
    t_load.wait()
    for j in range(1, Q):
        mine = tokall.at[own_t]
        send(remote(mine, mine, tok_send.at[j], tok_recv.at[seq], span, (seq + j) % Q))

    def project(step):
        zz = at_z(order[step])
        rows = pl.ds(pl.multiple_of(zz * 4 * R, 4 * R), 4 * R)
        for xx in range(2):
            from_c(zz, xx).wait_recv()

        def tile(i, carry):
            j = i // Q
            trows = pl.ds(pl.multiple_of((i % Q) * T, T), T)
            part = mm(
                tokall[trows, rows], wbuf[rows, pl.ds(pl.multiple_of(j * hcols, 128), hcols)]
            )
            if step == 0:
                acc[j, trows] = part
            elif step == Z - 1:
                qkv[j, trows] = (acc[j, trows] + part).astype(BF16)
            else:
                acc[j, trows] += part
            return carry

        lax.fori_loop(0, 3 * Q, tile, 0)

    for step in range(Z):
        if step + 1 < Z:
            zn = at_z(order[step + 1])
            b = block(zn, x, c)
            remote(b, b, z_send.at[1], z_recv.at[zn], zn * 4 + x * 2 + c, seq).wait_recv()
            send(to_x(zn))
            send(to_c(zn, x))
        zz = at_z(order[step])
        from_x(zz).wait_recv()
        send(to_c(zz, 1 - x))
        if step == 1:
            for j in range(1, Q):
                theirs = tokall.at[pl.ds(pl.multiple_of(((seq + j) % Q) * T, T), T)]
                remote(
                    theirs, theirs, tok_send.at[j], tok_recv.at[(seq + j) % Q], span, (seq + j) % Q
                ).wait_recv()
        if step >= 1:
            project(step - 1)
    project(Z - 1)

    def self_attend(owner, target):
        trows = pl.ds(pl.multiple_of(owner * T, T), T)

        def pair(p, carry):
            cols = pl.ds(pl.multiple_of(p * PAIR, PAIR), PAIR)
            num, tot, _ = pair_attend(qkv[0, trows, cols], qkv[1, :, cols], qkv[2, :, cols])
            target[:, cols] = (num / tot).astype(BF16)
            return carry

        lax.fori_loop(0, hcols // PAIR, pair, 0)

    for j in range(1, Q):
        owner = (seq + j) % Q
        self_attend(owner, attn_tx.at[j])
        send(remote(attn_tx.at[j], attn.at[seq], at_send.at[j], at_recv.at[seq], span, owner))
    self_attend(seq, attn.at[seq])
    wo_load.wait()
    NT = 256

    def out_part(j_seq, first):
        wrows = pl.ds(pl.multiple_of(j_seq * hcols, hcols), hcols)

        def tile(i, carry):
            cols = pl.ds(pl.multiple_of(i * NT, NT), NT)
            part = mm(attn[j_seq], wout[wrows, cols])
            if first:
                res[:, cols] = tokall[own_t, cols].astype(F32) + part
            else:
                res[:, cols] += part
            return carry

        lax.fori_loop(0, D // NT, tile, 0)

    out_part(seq, True)
    for j in range(1, Q):
        owner = (seq + j) % Q
        remote(
            attn_tx.at[j], attn.at[owner], at_send.at[j], at_recv.at[owner], span, owner
        ).wait_recv()
        out_part(owner, False)
    LT = 64

    def norm(i, carry):
        rows = pl.ds(pl.multiple_of(i * LT, LT), LT)
        r = res[rows]
        center = r - jnp.mean(r, -1, keepdims=True)
        spread = jnp.mean(center * center, -1, keepdims=True)
        enc_ref[rows] = (
            center * lax.rsqrt(spread + 1e-05) * gain_ref[...] + bias_ref[...]
        ).astype(BF16)
        return carry

    lax.fori_loop(0, T // LT, norm, 0)

    for copy in wc_loads:
        copy.wait()

    def kv_copy(g, at):
        return remote(
            kv_tx.at[g], kv.at[pl.ds(pl.multiple_of(at * T, T), T)],
            kv_send.at[g], kv_recv.at[at], base + g, seq,
        )

    def kv_step(i, carry):
        g = (member + i) % G
        kv_tx[g] = mm(enc_ref[...], wc[g]).astype(BF16)
        kv_copy(g, member).start()
        return carry

    lax.fori_loop(1, G, kv_step, 0)
    kv[pl.ds(pl.multiple_of(member * T, T), T)] = mm(enc_ref[...], wc[member]).astype(BF16)
    q_load.wait()

    def kv_wait(i, carry):
        g = (member + i) % G
        kv_copy(g, g).wait_recv()
        return carry

    lax.fori_loop(1, G, kv_wait, 0)

    BQ = max(own_rows, min(256, NQ))
    nb = BQ // own_rows
    lane = lax.broadcasted_iota(jnp.int32, (own_rows, PAIR), 1)
    row = lax.broadcasted_iota(jnp.int32, (own_rows, PAIR), 0)
    diagonal = (lane % DH) == row

    def part_copies(r, s):
        to = r * Q + s
        return (
            remote(o_tx.at[r], o_rx.at[flat], o_send.at[to], o_recv.at[flat], r, s),
            remote(l_tx.at[r], l_rx.at[flat], l_send.at[to], l_recv.at[flat], r, s),
        )

    def cross(i, carry):
        rows = pl.ds(pl.multiple_of(i * BQ, BQ), BQ)
        num, tot, peak = pair_attend(qc[rows], kv[:, :PAIR], kv[:, PAIR:])
        part = (num / tot).astype(BF16)
        lse = peak + jnp.log(tot)
        for b in range(nb):
            r = i * nb + b
            stat = jnp.sum(
                jnp.where(diagonal, lse[b * own_rows:(b + 1) * own_rows], 0.0), 0, keepdims=True
            )
            stat = jnp.broadcast_to(stat, (8, PAIR))
            o_tx[r] = part[b * own_rows:(b + 1) * own_rows]
            l_tx[r] = stat

            @pl.when(r == span)
            def _():
                o_rx[flat] = part[b * own_rows:(b + 1) * own_rows]
                l_rx[flat] = stat

            for s in range(Q):
                @pl.when(r * Q + s != flat)
                def _():
                    for copy in part_copies(r, s):
                        copy.start()
        return carry

    lax.fori_loop(0, NQ // BQ, cross, 0)

    def part_wait(i, carry):
        src = (flat + i) % n
        r = src // Q
        s = src % Q
        remote(o_tx.at[r], o_rx.at[src], o_send.at[src], o_recv.at[src], r, s).wait_recv()
        remote(l_tx.at[r], l_rx.at[src], l_send.at[src], l_recv.at[src], r, s).wait_recv()
        return carry

    lax.fori_loop(1, n, part_wait, 0)

    low = lane < DH

    def merge(g, carry):
        sources = [(a * G + g) * Q + s for a in range(S // G) for s in range(Q)]
        stats = [l_rx[src][0:1] for src in sources]
        top = functools.reduce(jnp.maximum, stats)
        weights = [jnp.exp(v - top) for v in stats]
        whole = functools.reduce(jnp.add, weights)
        total = jnp.zeros((own_rows, PAIR), F32)
        for src, weight in zip(sources, weights):
            spread = jnp.where(diagonal, weight / whole, 0.0)
            left = jnp.sum(jnp.where(low, spread, 0.0), 1, keepdims=True)
            right = jnp.sum(jnp.where(low, 0.0, spread), 1, keepdims=True)
            total += o_rx[src].astype(F32) * jnp.where(low, left, right)
        out_ref[:, pl.ds(pl.multiple_of(g * PAIR, PAIR), PAIR)] = total.astype(BF16)
        return carry

    lax.fori_loop(0, G, merge, 0)

    for copy in sent:
        copy.wait_send()

    def kv_sent(i, carry):
        kv_copy((member + i) % G, member).wait_send()
        return carry

    lax.fori_loop(1, G, kv_sent, 0)

    def part_sent(i, carry):
        to = (flat + i) % n
        for copy in part_copies(to // Q, to % Q):
            copy.wait_send()
        return carry

    lax.fori_loop(1, n, part_sent, 0)


def solution(mesh):
    S = mesh.shape["span"]
    Q = mesh.shape["seq"]

    def per_device(tokens, w_qkv, w_out, w_cross, ln_gain, ln_bias, queries):
        T, D = tokens.shape
        NQ = queries.shape[0]
        hcols = D // Q
        Z = S // 4
        G = D // PAIR
        own_rows = NQ // S
        any_spec = pl.BlockSpec(memory_space=pl.ANY)
        vmem_spec = pl.BlockSpec(memory_space=pltpu.VMEM)
        dma = pltpu.SemaphoreType.DMA
        n = S * Q
        return pl.pallas_call(
            functools.partial(kernel, S, Q, NQ),
            out_shape=(
                jax.ShapeDtypeStruct((T, D), BF16),
                jax.ShapeDtypeStruct((own_rows, D), BF16),
            ),
            in_specs=[any_spec] * 4 + [vmem_spec] * 2 + [any_spec],
            out_specs=(vmem_spec, vmem_spec),
            scratch_shapes=[
                pltpu.VMEM((D, 3 * hcols), BF16),
                pltpu.VMEM((Q * T, D), BF16),
                pltpu.VMEM((3, Q * T, hcols), F32),
                pltpu.VMEM((3, Q * T, hcols), BF16),
                pltpu.VMEM((D, D), BF16),
                pltpu.VMEM((G, D, 2 * PAIR), BF16),
                pltpu.VMEM((NQ, PAIR), BF16),
                pltpu.VMEM((Q, T, hcols), BF16),
                pltpu.VMEM((Q, T, hcols), BF16),
                pltpu.VMEM((T, D), F32),
                pltpu.VMEM((G, T, 2 * PAIR), BF16),
                pltpu.VMEM((G * T, 2 * PAIR), BF16),
                pltpu.VMEM((S, own_rows, PAIR), BF16),
                pltpu.VMEM((S, 8, PAIR), F32),
                pltpu.VMEM((n, own_rows, PAIR), BF16),
                pltpu.VMEM((n, 8, PAIR), F32),
                dma((6 + 2 * G,)),
                dma((Z,)), dma((Z,)), dma((Z,)), dma((Z,)), dma((2 * Z,)), dma((2 * Z,)),
                dma((Q,)), dma((Q,)), dma((Q,)), dma((Q,)), dma((G,)), dma((G,)),
                dma((n,)), dma((n,)), dma((n,)), dma((n,)),
            ],
            compiler_params=pltpu.CompilerParams(
                collective_id=0, has_side_effects=True, vmem_limit_bytes=56 << 20
            ),
        )(tokens, w_qkv, w_out, w_cross, ln_gain.reshape(1, D), ln_bias.reshape(1, D), queries)

    in_specs = (P(("span", "seq"), None), P("span", None), P(), P(), P(), P(), P())
    out_specs = (P(("span", "seq"), None), P("span", None))
    return jax.shard_map(
        per_device, mesh=mesh, in_specs=in_specs, out_specs=out_specs, check_vma=False
    )
```

time: 456 us -> 88.3 us (0.19); the launches traced: 451 us -> 88.1 us
  waiting for transfers between devices: 329 us -> 0 us
  Pallas kernels: 0 us -> 84 us
  matrix products: 35.1 us -> 0 us
  blocking collectives: 27.2 us -> 0 us
  local copies, waits for them, and re-layouts: 29 us -> 3.44 us
  between operations: 13.9 us -> 0.64 us
  other arithmetic: 12.8 us -> 0 us
    psum x1 -> x0, waiting for transfers between devices: 141 us -> none  [per_device(): summed, sum_total = lax.psum((numerator, cross_total), ('span', 'seq'))]
    pmax x1 -> x0, waiting for transfers between devices: 121 us -> none  [per_device(): cross_peak = lax.pmax(local_peak, ('span', 'seq'))]
    pallas_call x0 -> x1, Pallas kernels: none -> 84 us  [per_device(): pl.pallas_call(functools.partial(kernel, S, Q, NQ), out_shape=(jax.ShapeD...]
    all_gather x1 -> x0, waiting for transfers between devices: 62.9 us -> none  [per_device(): lax.all_gather(w_qkv, 'span', axis=0, tiled=True)]
    dot_general x7 -> x0, matrix products: 35.1 us -> none  [the longest x1 10.7 us: per_device(): jnp.einsum('qhk,khd->qhd', cross_powers.astype(jnp.bfloat16), cross_value...]
    all_to_all x1 -> x0, blocking collectives: 27.2 us -> none  [per_device(): lax.all_to_all(projected, 'seq', split_axis=2, concat_axis=0, tiled=True)]
    reduce_sum x3 -> x0, other arithmetic: 10.9 us -> none  [the longest x1 9.28 us: per_device(): cross_total = jnp.sum(cross_powers, -1)]
    reshape x2 -> x0, local copies, waits for them, and re-layouts: 8.14 us -> none  [the longest x1 5.38 us: per_device(): numerator = numerator.reshape(query_count, model_width)]
  transfers between devices with their start and end apart: 4 -> 0, of which waited for: 4 -> 0; matrix products, arithmetic and copies ran while one was open for 1% -> 0% of each run, Pallas kernels for 0% -> 0%
where the time goes in v1:
time: 88.3 us; the launch traced here: 88.1 us
  Pallas kernels  84 us (95%)
  local copies, waits for them, and re-layouts  3.44 us (4%)
    pallas_call x1, Pallas kernels, per_device(): pl.pallas_call(functools.partial(kernel, S, Q, NQ), out_shape=(jax.ShapeD...  84 us
    unnamed x2, local copies, waits for them, and re-layouts  3.44 us

profile of v1, /device:TPU:27, one launch (start us, length us, event | category | flops | bytes accessed | tf_op | source)
XLA Modules:
  0.0 88.1 jit_solution(9346817788803544187)
XLA Ops:
  0.6 84.0 %shard_map.86 = (bf16[256,1024]{1,0:T(8,128)(2,1)}, bf16[64,1024]{1,0:T(8,128)(2,1)}) custom-call(bf16[256,1024]{1,0:T(8,128)(2,1)} %tokens_ref.1, bf16[64,3072]{1,0:T(8,128)(2,1)} %wqkv_ref.1, bf16[1024,1024]{1,0:T(8,128)(2,1)} %wout_ref.1, bf16[1024,2048]{1,0:T(8,128)(2,1)} %wcross_ref.1, f32[1,1024]{1,0:T(1,128)} %bitcast.2, f32[1,1024]{1,0:T(1,128)} %bitcast.3, ...), custom_call_target="tpu_custom_call" | custom-call | tf_op jit(solution)/shard_map/pallas_call | solution.py:391
  84.6 1.9 %copy.11 = bf16[256,1024]{1,0:T(8,128)(2,1)} copy(bf16[256,1024]{1,0:T(8,128)(2,1)} %get-tuple-element.4) | data formatting | bytes 1048576
  86.5 1.6 %copy.12 = bf16[64,1024]{1,0:T(8,128)(2,1)} copy(bf16[64,1024]{1,0:T(8,128)(2,1)} %get-tuple-element.5) | data formatting | bytes 262144

commit v2 on v1

--- a/solution.py
+++ b/solution.py
@@ -49,7 +49,7 @@
     tokens_ref, wqkv_ref, wout_ref, wcross_ref, gain_ref, bias_ref, queries_ref,
     enc_ref, out_ref,
     wbuf, tokall, acc, qkv, wout, wc, qc, attn_tx, attn, res, kv_tx, kv, o_tx, l_tx, o_rx, l_rx,
-    local_sem, z_send, z_recv, x_send, x_recv, c_send, c_recv,
+    local_sem, r_send, l_out, z_recv, x_send, x_recv, c_send, c_recv,
     tok_send, tok_recv, at_send, at_recv, kv_send, kv_recv, o_send, o_recv, l_send, l_recv,
 ):
     T, D = tokens_ref.shape
@@ -89,14 +89,28 @@
     barrier = pltpu.get_barrier_semaphore()
     n = S * Q
 
-    def greet(i, carry):
-        other = (flat + i) % n
+    def greet(to_span, to_seq):
         pl.semaphore_signal(
-            barrier, inc=1, device_id={"span": other // Q, "seq": other % Q}, device_id_type=MESH
-        )
-        return carry
-
-    lax.fori_loop(1, n, greet, 0)
+            barrier, inc=1, device_id={"span": to_span, "seq": to_seq}, device_id_type=MESH
+        )
+
+    x_peer = z * 4 + (1 - x) * 2 + c
+    c_peer = z * 4 + x * 2 + (1 - c)
+    greet(c_peer, seq)
+    greet(x_peer, seq)
+    for j in range(1, Q):
+        greet(span, (seq + j) % Q)
+    has_right = z < Z - 1
+    has_left = z > 0
+
+    @pl.when(has_right)
+    def _():
+        greet(span + 4, seq)
+
+    @pl.when(has_left)
+    def _():
+        greet(span - 4, seq)
+
     wo_load = load(wout_ref, wout)
     wc_loads = []
     for g in range(G):
@@ -110,7 +124,8 @@
     q_load = load(queries_ref.at[:, pl.ds(pl.multiple_of(member * PAIR, PAIR), PAIR)], qc)
     for copy in w_loads:
         copy.wait()
-    pl.semaphore_wait(barrier, n - 1)
+    sides = (z + Z - 2) // (Z - 1) + (2 * Z - 3 - z) // (Z - 1)
+    pl.semaphore_wait(barrier, Q + 1 + sides)
 
     def remote(src, dst, ssem, rsem, to_span, to_seq):
         return pltpu.make_async_remote_copy(
@@ -121,53 +136,48 @@
     def block(zz, xx, cc):
         return wbuf.at[pl.ds(pl.multiple_of((zz * 4 + xx * 2 + cc) * R, R), R)]
 
-    x_peer = z * 4 + (1 - x) * 2 + c
-    c_peer = z * 4 + x * 2 + (1 - c)
     sent = []
 
     def send(copy):
         copy.start()
         sent.append(copy)
 
-    def to_x(zz):
+    def by_x(zz, xx):
+        b = block(zz, xx, c)
+        return remote(b, b, x_send.at[zz], x_recv.at[zz], x_peer, seq)
+
+    def by_c(zz, xx, cc):
+        b = block(zz, xx, cc)
+        return remote(b, b, c_send.at[zz * 2 + xx], c_recv.at[zz * 2 + xx], c_peer, seq)
+
+    def by_right(zz):
         b = block(zz, x, c)
-        return remote(b, b, x_send.at[zz], x_recv.at[zz], x_peer, seq)
-
-    def from_x(zz):
-        b = block(zz, 1 - x, c)
-        return remote(b, b, x_send.at[zz], x_recv.at[zz], x_peer, seq)
-
-    def to_c(zz, xx):
-        b = block(zz, xx, c)
-        return remote(b, b, c_send.at[zz * 2 + xx], c_recv.at[zz * 2 + xx], c_peer, seq)
-
-    def from_c(zz, xx):
-        b = block(zz, xx, 1 - c)
-        return remote(b, b, c_send.at[zz * 2 + xx], c_recv.at[zz * 2 + xx], c_peer, seq)
-
-    def at_z(k):
-        return (z + k) % Z
-
-    order = [0]
-    for d in range(1, Z // 2 + 1):
-        for k in (d, Z - d):
-            if k not in order:
-                order.append(k)
-    send(to_x(z))
-    send(to_c(z, x))
-    for k in order[1:]:
-        b = block(z, x, c)
-        send(remote(b, b, z_send.at[k], z_recv.at[z], at_z(k) * 4 + x * 2 + c, seq))
-    t_load.wait()
-    for j in range(1, Q):
-        mine = tokall.at[own_t]
-        send(remote(mine, mine, tok_send.at[j], tok_recv.at[seq], span, (seq + j) % Q))
-
-    def project(step):
-        zz = at_z(order[step])
+        return remote(b, b, r_send.at[zz], z_recv.at[zz], span + 4, seq)
+
+    def by_left(zz):
+        b = block(zz, x, c)
+        return remote(b, b, l_out.at[zz], z_recv.at[zz], span - 4, seq)
+
+    def spread(zz, rightward, leftward):
+        if rightward:
+            @pl.when(has_right)
+            def _():
+                by_right(zz).start()
+        if leftward:
+            @pl.when(has_left)
+            def _():
+                by_left(zz).start()
+        by_x(zz, x).start()
+        by_c(zz, x, c).start()
+
+    def cross_over(zz):
+        by_x(zz, 1 - x).wait_recv()
+        by_c(zz, 1 - x, c).start()
+
+    def project(zz, first):
         rows = pl.ds(pl.multiple_of(zz * 4 * R, 4 * R), 4 * R)
         for xx in range(2):
-            from_c(zz, xx).wait_recv()
+            by_c(zz, xx, 1 - c).wait_recv()
 
         def tile(i, carry):
             j = i // Q
@@ -175,52 +185,83 @@
             part = mm(
                 tokall[trows, rows], wbuf[rows, pl.ds(pl.multiple_of(j * hcols, 128), hcols)]
             )
-            if step == 0:
+            if first:
                 acc[j, trows] = part
-            elif step == Z - 1:
-                qkv[j, trows] = (acc[j, trows] + part).astype(BF16)
             else:
                 acc[j, trows] += part
             return carry
 
         lax.fori_loop(0, 3 * Q, tile, 0)
 
-    for step in range(Z):
-        if step + 1 < Z:
-            zn = at_z(order[step + 1])
-            b = block(zn, x, c)
-            remote(b, b, z_send.at[1], z_recv.at[zn], zn * 4 + x * 2 + c, seq).wait_recv()
-            send(to_x(zn))
-            send(to_c(zn, x))
-        zz = at_z(order[step])
-        from_x(zz).wait_recv()
-        send(to_c(zz, 1 - x))
-        if step == 1:
+    spread(z, True, True)
+    t_load.wait()
+    for j in range(1, Q):
+        mine = tokall.at[own_t]
+        send(remote(mine, mine, tok_send.at[j], tok_recv.at[seq], span, (seq + j) % Q))
+
+    def at_distance(t, action):
+        @pl.when(z >= t)
+        def _():
+            action(z - t, True)
+
+        @pl.when(z + t < Z)
+        def _():
+            action(z + t, False)
+
+    def arrive(zz, from_left):
+        by_right(zz).wait_recv()
+        spread(zz, from_left, not from_left)
+
+    for t in range(Z):
+        if t + 1 < Z:
+            at_distance(t + 1, arrive)
+        if t == 0:
+            cross_over(z)
+        else:
+            at_distance(t, lambda zz, _: cross_over(zz))
+        if t == 1:
             for j in range(1, Q):
                 theirs = tokall.at[pl.ds(pl.multiple_of(((seq + j) % Q) * T, T), T)]
                 remote(
                     theirs, theirs, tok_send.at[j], tok_recv.at[(seq + j) % Q], span, (seq + j) % Q
                 ).wait_recv()
-        if step >= 1:
-            project(step - 1)
-    project(Z - 1)
-
-    def self_attend(owner, target):
+            project(z, True)
+        elif t > 1:
+            at_distance(t - 1, lambda zz, _: project(zz, False))
+    at_distance(Z - 1, lambda zz, _: project(zz, False))
+
+    def round_off(i, carry):
+        j = i // Q
+        trows = pl.ds(pl.multiple_of((i % Q) * T, T), T)
+        qkv[j, trows] = acc[j, trows].astype(BF16)
+        return carry
+
+    lax.fori_loop(0, 3 * Q, round_off, 0)
+
+    def pair_copy(j, p, at, owner):
+        cols = pl.ds(pl.multiple_of(p * PAIR, PAIR), PAIR)
+        return remote(
+            attn_tx.at[j, :, cols], attn.at[at, :, cols], at_send.at[j, p], at_recv.at[at, p],
+            span, owner,
+        )
+
+    def self_attend(j, owner, target):
         trows = pl.ds(pl.multiple_of(owner * T, T), T)
 
         def pair(p, carry):
             cols = pl.ds(pl.multiple_of(p * PAIR, PAIR), PAIR)
             num, tot, _ = pair_attend(qkv[0, trows, cols], qkv[1, :, cols], qkv[2, :, cols])
             target[:, cols] = (num / tot).astype(BF16)
+            if j:
+                pair_copy(j, p, seq, owner).start()
             return carry
 
         lax.fori_loop(0, hcols // PAIR, pair, 0)
 
     for j in range(1, Q):
         owner = (seq + j) % Q
-        self_attend(owner, attn_tx.at[j])
-        send(remote(attn_tx.at[j], attn.at[seq], at_send.at[j], at_recv.at[seq], span, owner))
-    self_attend(seq, attn.at[seq])
+        self_attend(j, owner, attn_tx.at[j])
+    self_attend(0, seq, attn.at[seq])
     wo_load.wait()
     NT = 256
 
@@ -241,9 +282,8 @@
     out_part(seq, True)
     for j in range(1, Q):
         owner = (seq + j) % Q
-        remote(
-            attn_tx.at[j], attn.at[owner], at_send.at[j], at_recv.at[owner], span, owner
-        ).wait_recv()
+        for p in range(hcols // PAIR):
+            pair_copy(j, p, owner, owner).wait_recv()
         out_part(owner, False)
     LT = 64
 
@@ -298,7 +338,8 @@
             remote(l_tx.at[r], l_rx.at[flat], l_send.at[to], l_recv.at[flat], r, s),
         )
 
-    def cross(i, carry):
+    def cross(step, carry):
+        i = (z + 1 + step) % (NQ // BQ)
         rows = pl.ds(pl.multiple_of(i * BQ, BQ), BQ)
         num, tot, peak = pair_attend(qc[rows], kv[:, :PAIR], kv[:, PAIR:])
         part = (num / tot).astype(BF16)
@@ -357,6 +398,21 @@
 
     for copy in sent:
         copy.wait_send()
+    for j in range(1, Q):
+        for p in range(hcols // PAIR):
+            pair_copy(j, p, seq, (seq + j) % Q).wait_send()
+    for zz in range(Z):
+        by_x(zz, x).wait_send()
+        for xx in range(2):
+            by_c(zz, xx, c).wait_send()
+
+        @pl.when(has_right & (z >= zz))
+        def _():
+            by_right(zz).wait_send()
+
+        @pl.when(has_left & (z <= zz))
+        def _():
+            by_left(zz).wait_send()
 
     def kv_sent(i, carry):
         kv_copy((member + i) % G, member).wait_send()
@@ -371,6 +427,11 @@
         return carry
 
     lax.fori_loop(1, n, part_sent, 0)
+
+
+def hand_over(enc_ref, part_ref, enc_out, part_out):
+    enc_out[...] = enc_ref[...]
+    part_out[...] = part_ref[...]
 
 
 def solution(mesh):
@@ -388,7 +449,7 @@
         vmem_spec = pl.BlockSpec(memory_space=pltpu.VMEM)
         dma = pltpu.SemaphoreType.DMA
         n = S * Q
-        return pl.pallas_call(
+        results = pl.pallas_call(
             functools.partial(kernel, S, Q, NQ),
             out_shape=(
                 jax.ShapeDtypeStruct((T, D), BF16),
@@ -414,14 +475,20 @@
                 pltpu.VMEM((n, own_rows, PAIR), BF16),
                 pltpu.VMEM((n, 8, PAIR), F32),
                 dma((6 + 2 * G,)),
-                dma((Z,)), dma((Z,)), dma((Z,)), dma((Z,)), dma((2 * Z,)), dma((2 * Z,)),
-                dma((Q,)), dma((Q,)), dma((Q,)), dma((Q,)), dma((G,)), dma((G,)),
+                dma((Z,)), dma((Z,)), dma((Z,)), dma((Z,)), dma((Z,)), dma((2 * Z,)), dma((2 * Z,)),
+                dma((Q,)), dma((Q,)), dma((Q, hcols // PAIR)), dma((Q, hcols // PAIR)), dma((G,)), dma((G,)),
                 dma((n,)), dma((n,)), dma((n,)), dma((n,)),
             ],
             compiler_params=pltpu.CompilerParams(
                 collective_id=0, has_side_effects=True, vmem_limit_bytes=56 << 20
             ),
         )(tokens, w_qkv, w_out, w_cross, ln_gain.reshape(1, D), ln_bias.reshape(1, D), queries)
+        return pl.pallas_call(
+            hand_over,
+            out_shape=tuple(jax.ShapeDtypeStruct(r.shape, r.dtype) for r in results),
+            in_specs=[vmem_spec] * 2,
+            out_specs=(vmem_spec, vmem_spec),
+        )(*results)
 
     in_specs = (P(("span", "seq"), None), P("span", None), P(), P(), P(), P(), P())
     out_specs = (P(("span", "seq"), None), P("span", None))

time: 88.3 us -> 75.4 us (0.85)
  Pallas kernels: 84 us -> 74.3 us
  local copies, waits for them, and re-layouts: 3.44 us -> 0 us
    pallas_call x1, Pallas kernels: 84 us -> 72.4 us  [per_device(): pl.pallas_call(functools.partial(kernel, S, Q, NQ), out_shape=(jax.ShapeD...]
    unnamed x2 -> x0, local copies, waits for them, and re-layouts: 3.44 us -> none
    pallas_call x0 -> x1, Pallas kernels: none -> 1.93 us  [per_device(): pl.pallas_call(hand_over, out_shape=tuple((jax.ShapeDtypeStruct(r.shape,...]
where the time goes in v2:
time: 75.4 us; the launch traced here: 75 us
  Pallas kernels  74.3 us (99%)
    pallas_call x1, Pallas kernels, per_device(): pl.pallas_call(functools.partial(kernel, S, Q, NQ), out_shape=(jax.ShapeD...  72.4 us
    pallas_call x1, Pallas kernels, per_device(): pl.pallas_call(hand_over, out_shape=tuple((jax.ShapeDtypeStruct(r.shape,...  1.93 us

profile of v2, /device:TPU:27, one launch (start us, length us, event | category | flops | bytes accessed | tf_op | source)
XLA Modules:
  0.0 75.0 jit_solution(3450770655656175905)
XLA Ops:
  0.6 72.4 %shard_map.86 = (bf16[256,1024]{1,0:T(8,128)(2,1)}, bf16[64,1024]{1,0:T(8,128)(2,1)}) custom-call(bf16[256,1024]{1,0:T(8,128)(2,1)} %tokens_ref.1, bf16[64,3072]{1,0:T(8,128)(2,1)} %wqkv_ref.1, bf16[1024,1024]{1,0:T(8,128)(2,1)} %wout_ref.1, bf16[1024,2048]{1,0:T(8,128)(2,1)} %wcross_ref.1, f32[1,1024]{1,0:T(1,128)} %bitcast.2, f32[1,1024]{1,0:T(1,128)} %bitcast.3, ...), custom_call_target="tpu_custom_call" | custom-call | tf_op jit(solution)/shard_map/pallas_call | solution.py:452
  73.0 1.9 %shard_map.87 = (bf16[256,1024]{1,0:T(8,128)(2,1)}, bf16[64,1024]{1,0:T(8,128)(2,1)}) custom-call(bf16[256,1024]{1,0:T(8,128)(2,1)} %get-tuple-element.4.enc_ref, bf16[64,1024]{1,0:T(8,128)(2,1)} %get-tuple-element.5.part_ref), custom_call_target="tpu_custom_call" | custom-call | tf_op jit(solution)/shard_map/pallas_call | solution.py:486
